TPU v7x, 32 devices: a whole 2x2x4 slice. The times are simulated.
32 devices in a mesh: shot: 2 (over x), gx: 16 (over z, y, core).
Axes of the slice: x: 2, y: 2, z: 4, core: 2. Of those that a mesh axis runs over, the one named last changes fastest.
Arguments:
- waves_now: float32 [2, 1024, 64, 128], P(None, ('shot', 'gx')), parts along dimension 1, may hold values from -6 to 6
- waves_prev: float32 [2, 1024, 64, 128], P(None, ('shot', 'gx')), parts along dimension 1, may hold values from -6 to 6
- epsilon: bfloat16 [512, 64, 128], P('gx'), may hold values from 0.049804688 to 0.3984375
- tilt: bfloat16 [512, 64, 128], P('gx'), may hold values from -3.140625 to 3.140625
- azimuth: bfloat16 [512, 64, 128], P('gx'), may hold values from -3.140625 to 3.140625
- courant: bfloat16 [512, 64, 128], P('gx'), may hold values from 0.029907227 to 0.099609375
- lag_offsets: int32 [32], replicated, may hold values from -16 to 15
- table_index: int32 [128], replicated, may hold values from 0 to 3
- lag_tables: bfloat16 [4, 32, 32], replicated, may hold values from -1 to 1
Outputs:
- angle_image: bfloat16 [32, 8192, 256], P(None, ('shot', 'gx')), parts along dimension 1
There are 2 independent parts, one for each index of `shot`. A program takes and returns all parts, laid end to end along the dimension named above; an argument that names none is the same for every part. Nothing has to cross between parts.
All inputs are finite; a program needn't handle non-finite values.
Results may differ from a plain program's by a relative error of at most 0.0049.
Values may be sent and summed in bfloat16 or wider, within the bound.
A program may use at most 64 MiB of HBM per device.

v0:
```python
import functools
import jax
import jax.numpy as jnp
from jax import lax
from jax.experimental import pallas as pl
from jax.experimental.pallas import tpu as pltpu
from jax.sharding import PartitionSpec as P

STEPS = 4
LAG_REACH = 16
PAD = 8
F32 = jnp.float32
SEND = jnp.bfloat16


def sin_cos(x):
    h = x * 0.5
    h2 = h * h
    s = h2 * 2.609020676498479e-06 + (-0.00019811149207883466)
    s = s * h2 + 0.008333088613525165
    s = s * h2 + (-0.16666660477455342)
    s = s * h2 * h + h
    c = h2 * (-2.607799327383753e-07) + 2.4761934264809493e-05
    c = c * h2 + (-0.0013888404392126607)
    c = c * h2 + 0.04166664079116777
    c = c * h2 + (-0.4999999955092854)
    c = c * h2 + 1.0
    s2 = s + s
    return s2 * c, 1.0 - s2 * s


def wave_kernel(
    n, jr, cols_per, now_hbm, prev_hbm, eps_hbm, tilt_hbm, azi_hbm, cou_hbm, cols_ref,
    buf0, buf1, dz, dy, part, eps, tilt, azi, cou, coef, pair, snap, snap_send, sendbuf, halo,
    in_sems, hs_sems, hr_sems, as_sems, ar_sems,
):
    width = eps.shape[0]
    ny = eps.shape[1]
    nz = eps.shape[2]
    rows = pl.ds(PAD, ny)
    up_rows = pl.ds(PAD + 1, ny)
    dn_rows = pl.ds(PAD - 1, ny)
    me = lax.axis_index("gx")
    has_low = me > 0
    has_high = me < n - 1
    bufs = (buf0, buf1)

    copies = [
        pltpu.make_async_copy(tilt_hbm, tilt, in_sems.at[0]),
        pltpu.make_async_copy(azi_hbm, azi, in_sems.at[1]),
        pltpu.make_async_copy(eps_hbm, eps, in_sems.at[2]),
        pltpu.make_async_copy(cou_hbm, cou, in_sems.at[3]),
        pltpu.make_async_copy(now_hbm, buf0.at[:, pl.ds(1, width), rows, :], in_sems.at[4]),
        pltpu.make_async_copy(prev_hbm, buf1.at[:, pl.ds(1, width), rows, :], in_sems.at[5]),
    ]
    for copy in copies:
        copy.start()

    barrier = pltpu.get_barrier_semaphore()

    def greet(k, carry):
        pl.semaphore_signal(
            barrier, inc=1, device_id={"gx": lax.rem(me + k, n)},
            device_id_type=pl.DeviceIdType.MESH,
        )
        return carry

    lax.fori_loop(1, n, greet, 0)

    zero_rows = jnp.zeros((2, width + 2, PAD, nz), F32)
    for ref in (buf0, buf1, dz):
        ref[:, :, pl.ds(0, PAD), :] = zero_rows
        ref[:, :, pl.ds(PAD + ny, PAD), :] = zero_rows
    zero_plane = jnp.zeros((2, ny, nz), F32)
    for plane in (0, width + 1):
        for ref in (buf0, buf1):
            ref[:, plane, rows, :] = zero_plane
        dz[:, plane, rows, :] = zero_plane
        dy[:, plane] = zero_plane

    pl.semaphore_wait(barrier, n - 1)

    def halo_copy(step, side):
        if step == 0:
            src = now_hbm.at[:, 0 if side == 0 else width - 1]
        else:
            src = sendbuf.at[step - 1, side]
        return pltpu.make_async_remote_copy(
            src_ref=src,
            dst_ref=halo.at[step, 1 - side],
            send_sem=hs_sems.at[step, side],
            recv_sem=hr_sems.at[step, 1 - side],
            device_id={"gx": me - 1 if side == 0 else me + 1},
            device_id_type=pl.DeviceIdType.MESH,
        )

    def halo_arrived(step, side):
        return pltpu.make_async_remote_copy(
            src_ref=sendbuf.at[0, side],
            dst_ref=halo.at[step, side],
            send_sem=hs_sems.at[step, side],
            recv_sem=hr_sems.at[step, side],
            device_id={"gx": me - 1 if side == 0 else me + 1},
            device_id_type=pl.DeviceIdType.MESH,
        )

    def send_halo(step):
        @pl.when(has_low)
        def _():
            halo_copy(step, 0).start()

        @pl.when(has_high)
        def _():
            halo_copy(step, 1).start()

    send_halo(0)

    for copy in copies[:4]:
        copy.wait()

    def make_coef(x, carry):
        theta_s, theta_c = sin_cos(tilt[x].astype(F32))
        alpha_s, alpha_c = sin_cos(azi[x].astype(F32))
        speed = cou[x].astype(F32)
        e2 = eps[x].astype(F32) * 2.0
        scaled = speed * e2
        base = speed + scaled
        nx = theta_s * alpha_c
        nyy = theta_s * alpha_s
        sx = scaled * nx
        sy = scaled * nyy
        scz = scaled * theta_c
        mxx = base - sx * nx
        myy = base - sy * nyy
        mzz = base - scz * theta_c
        coef[0, x] = mxx
        coef[1, x] = myy
        coef[2, x] = mzz
        coef[3, x] = -0.5 * (sx * nyy)
        coef[4, x] = -0.5 * (scz * nx)
        coef[5, x] = -0.5 * (scz * nyy)
        coef[6, x] = 2.0 - 2.0 * (mxx + myy + mzz)
        return carry

    lax.fori_loop(0, width, make_coef, 0)
    for copy in copies[4:]:
        copy.wait()

    chunk = 16
    starts = range(0, ny, chunk)

    def z_shifts(p):
        lane = lax.broadcasted_iota(jnp.int32, p.shape, 1)
        up = jnp.where(lane == nz - 1, 0.0, pltpu.roll(p, nz - 1, axis=1))
        dn = jnp.where(lane == 0, 0.0, pltpu.roll(p, 1, axis=1))
        return up, dn

    def turns(now, x, y):
        return [z_shifts(now[f, x, pl.ds(PAD + y, chunk), :]) for f in range(2)]

    def own_rows(now, x, y, turned):
        here = pl.ds(y, chunk)
        c1, c2, c6 = [coef[k, x - 1, here, :] for k in (1, 2, 6)]
        for f in range(2):
            p = now[f, x, pl.ds(PAD + y, chunk), :]
            pu = now[f, x, pl.ds(PAD + y + 1, chunk), :]
            pd = now[f, x, pl.ds(PAD + y - 1, chunk), :]
            up, dn = turned[f]
            part[f, x, here, :] = c6 * p + c1 * (pu + pd) + c2 * (up + dn)
            dz[f, x, pl.ds(PAD + y, chunk), :] = up - dn
            dy[f, x, here, :] = pu - pd

    def own_plane(now, x):
        for y in starts:
            own_rows(now, x, y, turns(now, x, y))

    def update(now, prv, x, picked=starts):
        for y in picked:
            here = pl.ds(y, chunk)
            mid = pl.ds(PAD + y, chunk)
            c0, c3, c4, c5 = [coef[k, x - 1, here, :] for k in (0, 3, 4, 5)]
            for f in range(2):
                acc = part[f, x, here, :] - prv[f, x, mid, :]
                acc += c0 * (now[f, x + 1, mid, :] + now[f, x - 1, mid, :])
                acc += c3 * (dy[f, x + 1, here, :] - dy[f, x - 1, here, :])
                acc += c4 * (dz[f, x + 1, mid, :] - dz[f, x - 1, mid, :])
                acc += c5 * (
                    dz[f, x, pl.ds(PAD + y + 1, chunk), :] - dz[f, x, pl.ds(PAD + y - 1, chunk), :]
                )
                prv[f, x, mid, :] = acc

    for step in range(STEPS):
        now, prv = bufs[step % 2], bufs[(step + 1) % 2]
        for x in (1, 2, 3):
            own_plane(now, x)

        def interior(x, carry, now=now, prv=prv):
            turned = turns(now, x + 2, 0)
            for y in starts:
                update(now, prv, x, (y,))
                ahead = turns(now, x + 2, y + chunk) if y + chunk < ny else None
                own_rows(now, x + 2, y, turned)
                turned = ahead
            return carry

        lax.fori_loop(2, width - 1, interior, 0)
        update(now, prv, width - 1)

        for side, plane, edge, has in (
            (0, 0, 1, has_low), (1, width + 1, width, has_high),
        ):
            @pl.when(has)
            def _(side=side, plane=plane, now=now, step=step):
                halo_arrived(step, side).wait_recv()
                for f in range(2):
                    p = halo[step, side, f]
                    now[f, plane, rows, :] = p
                    up, dn = z_shifts(p)
                    dz[f, plane, rows, :] = up - dn
                for f in range(2):
                    dy[f, plane] = now[f, plane, up_rows, :] - now[f, plane, dn_rows, :]

            update(now, prv, edge)
            if step < STEPS - 1:
                for f in range(2):
                    sendbuf[step, side, f] = prv[f, edge, rows, :]

                @pl.when(has)
                def _(side=side, step=step):
                    halo_copy(step + 1, side).start()

    final = bufs[STEPS % 2]
    half = width // 2

    def make_snap(i, carry):
        for f in range(2):
            pair[f] = final[f, 2 * i + 1, rows, :] + final[f, 2 * i + 2, rows, :]
        for f in range(2):
            even = pair[f, pl.ds(0, ny // 2, stride=2), :]
            odd = pair[f, pl.ds(1, ny // 2, stride=2), :]
            snap[f, pl.ds(i, ny // 2, stride=half), :] = (even + odd) * 0.25
        return carry

    lax.fori_loop(0, half, make_snap, 0)

    span = jr * half

    def piece(target, source):
        start = pl.multiple_of(((target * cols_per) // nz) * half, half)
        return pltpu.make_async_remote_copy(
            src_ref=snap_send.at[:, pl.ds(start, span), :],
            dst_ref=cols_ref.at[source],
            send_sem=as_sems.at[target],
            recv_sem=ar_sems.at[source],
            device_id={"gx": target},
            device_id_type=pl.DeviceIdType.MESH,
        )

    snap_send[...] = snap[...].astype(SEND)

    def send_piece(k, carry):
        piece(lax.rem(me + k, n), me).start()
        return carry

    lax.fori_loop(n // 2, n, send_piece, 0)
    lax.fori_loop(1, n // 2, send_piece, 0)
    start = pl.multiple_of(((me * cols_per) // nz) * half, half)
    own = pltpu.make_async_copy(snap_send.at[:, pl.ds(start, span), :], cols_ref.at[me], in_sems.at[6])
    own.start()

    for step in range(STEPS):
        @pl.when(has_low)
        def _(step=step):
            halo_copy(step, 0).wait_send()

        @pl.when(has_high)
        def _(step=step):
            halo_copy(step, 1).wait_send()

    def wait_piece(k, carry):
        piece(lax.rem(me + k, n), me).wait_send()
        piece(lax.rem(me + k, n), lax.rem(me + k, n)).wait_recv()
        return carry

    lax.fori_loop(1, n, wait_piece, 0)
    own.wait()


def image_kernel(
    cols_per, jr, offsets, tables_at, cols_ref, tab_ref, out_ref, lines, wide, prods
):
    n = cols_ref.shape[0]
    half = cols_ref.shape[2] // jr
    nz = cols_ref.shape[3]
    full = n * half
    step = pl.program_id(0)
    tables = tab_ref.shape[0]
    angles = tab_ref.shape[1]
    lags = tab_ref.shape[2]

    @pl.when(step == 0)
    def _():
        for f in range(2):
            for j in range(jr):
                for t in range(full // nz):
                    per = nz // half
                    block = cols_ref[pl.ds(t * per, per), f, pl.ds(j * half, half), :]
                    block = block.reshape(nz, nz).astype(F32)
                    lines[f, j, :, pl.ds(t * nz, nz)] = block.T.astype(SEND)
        lag = lax.broadcasted_iota(jnp.int32, (lags, lags * 8), 0)
        col = lax.broadcasted_iota(jnp.int32, (lags, lags * 8), 1)
        spread = jnp.where(col // 8 == lag, 1.0, 0.0).astype(jnp.bfloat16)
        flat = tab_ref[...].reshape(tables * angles, lags)
        wide[...] = jnp.dot(flat, spread, preferred_element_type=F32).astype(jnp.bfloat16)

    me = lax.axis_index("gx")
    z0 = lax.rem(me * cols_per, nz)
    lane = lax.broadcasted_iota(jnp.int32, (16, nz), 1)
    tiles = full // nz
    ta = tables * angles
    sub = lax.broadcasted_iota(jnp.int32, (8, ta), 0)
    row_c = lax.rem(lax.broadcasted_iota(jnp.int32, (angles * 8, lags * 8), 0), 8)
    col_c = lax.rem(lax.broadcasted_iota(jnp.int32, (angles * 8, lags * 8), 1), 8)
    diagonal = row_c == col_c
    lane_ta = lax.broadcasted_iota(jnp.int32, (angles, 8, ta), 2)
    row_a = lax.broadcasted_iota(jnp.int32, (angles, 8, ta), 0)
    weights = []
    for q in range(2):
        row0 = z0 + step * 16 + q * 8
        chosen = jnp.zeros((8, ta), jnp.int32)
        for c in range(8):
            chosen = jnp.where(sub == c, tables_at[row0 + c], chosen)
        wanted = (chosen * angles)[None] + row_a
        pick = jnp.where(lane_ta == wanted, 1.0, 0.0).reshape(angles * 8, ta)
        dense = jnp.dot(pick.astype(jnp.bfloat16), wide[...], preferred_element_type=F32)
        weights.append(jnp.where(diagonal, dense, 0.0).astype(jnp.bfloat16))

    def moved(parts, d):
        if d == 0:
            return [part.astype(F32) for part in parts]
        turned = [pltpu.roll(part, d % nz, axis=1).astype(F32) for part in parts]
        zero = jnp.zeros((16, nz), F32)
        if d > 0:
            return [
                jnp.where(lane >= d, turned[t], turned[t - 1] if t else zero)
                for t in range(tiles)
            ]
        return [
            jnp.where(lane < nz + d, turned[t], turned[t + 1] if t + 1 < tiles else zero)
            for t in range(tiles)
        ]

    for j in range(jr):
        results = []
        row0 = pl.multiple_of(z0 + step * 16, 16)
        source = [lines[0, j, pl.ds(row0, 16), pl.ds(t * nz, nz)] for t in range(tiles)]
        receiver = [lines[1, j, pl.ds(row0, 16), pl.ds(t * nz, nz)] for t in range(tiles)]
        for d in range(-LAG_REACH, LAG_REACH):
            left, right = moved(source, d), moved(receiver, -d)
            for t in range(tiles):
                product = left[t] * right[t]
                for q in range(2):
                    prods[j * 2 + q, d + LAG_REACH, :, pl.ds(t * nz, nz)] = product[8 * q : 8 * q + 8]
        for q in range(2):
            slot = j * 2 + q
            lagged = jnp.concatenate(
                [prods[slot, offsets[h] + LAG_REACH] for h in range(lags)], axis=0
            ).astype(jnp.bfloat16)
            total = jnp.dot(weights[q], lagged, preferred_element_type=F32)
            results.append(total.reshape(angles, 8, full))
        both = jnp.concatenate(results, axis=1)
        out_ref[:, j] = both.astype(jnp.bfloat16)


def local(
    waves_now, waves_prev, epsilon, tilt, azimuth, courant, lag_offsets, table_index, lag_tables
):
    n = lax.axis_size("gx")
    width, ny, nz = epsilon.shape
    half = width // 2
    columns = (ny // 2) * nz
    cols_per = columns // n
    jr = max(1, cols_per // nz)
    full = n * half
    plane = (2, width + 2, ny + 2 * PAD, nz)
    dma = pltpu.SemaphoreType.DMA
    cols = pl.pallas_call(
        functools.partial(wave_kernel, n, jr, cols_per),
        out_shape=jax.ShapeDtypeStruct((n, 2, jr * half, nz), SEND),
        in_specs=[pl.BlockSpec(memory_space=pl.ANY)] * 6,
        out_specs=pl.BlockSpec(memory_space=pltpu.VMEM),
        scratch_shapes=[
            pltpu.VMEM(plane, F32),
            pltpu.VMEM(plane, F32),
            pltpu.VMEM(plane, F32),
            pltpu.VMEM((2, width + 2, ny, nz), F32),
            pltpu.VMEM((2, width + 2, ny, nz), F32),
            pltpu.VMEM((width, ny, nz), epsilon.dtype),
            pltpu.VMEM((width, ny, nz), tilt.dtype),
            pltpu.VMEM((width, ny, nz), azimuth.dtype),
            pltpu.VMEM((width, ny, nz), courant.dtype),
            pltpu.VMEM((7, width, ny, nz), F32),
            pltpu.VMEM((2, ny, nz), F32),
            pltpu.VMEM((2, (ny // 2) * half, nz), F32),
            pltpu.VMEM((2, (ny // 2) * half, nz), SEND),
            pltpu.VMEM((STEPS - 1, 2, 2, ny, nz), F32),
            pltpu.VMEM((STEPS, 2, 2, ny, nz), F32),
            dma((7,)),
            dma((STEPS, 2)),
            dma((STEPS, 2)),
            dma((n,)),
            dma((n,)),
        ],
        compiler_params=pltpu.CompilerParams(collective_id=0, has_side_effects=True),
        name="waves",
    )(waves_now, waves_prev, epsilon, tilt, azimuth, courant)

    angles, lags = lag_tables.shape[1:]
    tables = lag_tables.shape[0]
    cz = min(cols_per, nz)
    image = pl.pallas_call(
        functools.partial(image_kernel, cols_per, jr),
        grid=(cz // 16,),
        out_shape=jax.ShapeDtypeStruct((angles, jr, cz, full), jnp.bfloat16),
        in_specs=[
            pl.BlockSpec(memory_space=pltpu.SMEM),
            pl.BlockSpec(memory_space=pltpu.SMEM),
            pl.BlockSpec(memory_space=pltpu.VMEM),
            pl.BlockSpec(memory_space=pltpu.VMEM),
        ],
        out_specs=pl.BlockSpec((angles, jr, 16, full), lambda g: (0, 0, g, 0)),
        scratch_shapes=[
            pltpu.VMEM((2, jr, nz, full), SEND),
            pltpu.VMEM((tables * angles, lags * 8), jnp.bfloat16),
            pltpu.VMEM((jr * 2, 2 * LAG_REACH, 8, full), F32),
        ],
        name="image",
    )(lag_offsets, table_index, cols, lag_tables)
    return image.reshape(angles, cols_per, full)


def solution(mesh):
    wave = P(None, ("shot", "gx"), None, None)
    cell = P("gx", None, None)
    return jax.shard_map(
        local,
        mesh=mesh,
        in_specs=(wave, wave, cell, cell, cell, cell, P(), P(), P()),
        out_specs=P(None, ("shot", "gx"), None),
        check_vma=False,
    )
```

profile of v0, /device:TPU:0, one launch (start us, length us, event | category | flops | bytes accessed | tf_op | source)
XLA Modules:
  0.0 40.8 jit_solution(3767067084708682624)
XLA Ops:
  0.0 33.2 %waves.1.cols_ref = bf16[16,2,32,128]{3,2,1,0:T(8,128)(2,1)} custom-call(f32[2,32,64,128]{3,2,1,0:T(8,128)} %now_hbm.1, f32[2,32,64,128]{3,2,1,0:T(8,128)} %prev_hbm.1, bf16[32,64,128]{2,1,0:T(8,128)(2,1)} %eps_hbm.1, bf16[32,64,128]{2,1,0:T(8,128)(2,1)} %tilt_hbm.1, bf16[32,64,128]{2,1,0:T(8,128)(2,1)} %azi_hbm.1, bf16[32,64,128]{2,1,0:T(8,128)(2,1)} %cou_hbm.1), custom_call_target="tpu_custom_call" | custom-call | tf_op jit(solution)/shard_map/waves/pallas_call | solution.py:387
  33.2 7.7 %image.1 = bf16[32,2,128,256]{3,2,1,0:T(8,128)(2,1)} custom-call(s32[32]{0:T(128)} %offsets.1, s32[128]{0:T(128)} %tables_at.1, bf16[16,2,32,128]{3,2,1,0:T(8,128)(2,1)} %waves.1.cols_ref, bf16[4,32,32]{2,1,0:T(8,128)(2,1)} %tab_ref.1), custom_call_target="tpu_custom_call" | custom-call | tf_op jit(solution)/shard_map/image/pallas_call | solution.py:421
where the time goes:
time: 41 us; the launch traced here: 40.8 us
  Pallas kernels  40.8 us (100%)
    pallas_call x1, Pallas kernels, local(): pl.pallas_call(functools.partial(wave_kernel, n, jr, cols_per), out_shape...  33.2 us
    pallas_call x1, Pallas kernels, local(): pl.pallas_call(functools.partial(image_kernel, cols_per, jr), grid=(cz //...  7.66 us

commit v1 on v0

v1 whole, which is shorter than its diff:
```python
import functools
import jax
import jax.numpy as jnp
from jax import lax
from jax.experimental import pallas as pl
from jax.experimental.pallas import tpu as pltpu
from jax.sharding import PartitionSpec as P

STEPS = 4
LAG_REACH = 16
PAD = 8
ROWS = 8
EDGE = 32
GROUPS = 4
F32 = jnp.float32
SEND = jnp.bfloat16


def sin_cos(x):
    h = x * 0.5
    h2 = h * h
    s = h2 * 2.609020676498479e-06 + (-0.00019811149207883466)
    s = s * h2 + 0.008333088613525165
    s = s * h2 + (-0.16666660477455342)
    s = s * h2 * h + h
    c = h2 * (-2.607799327383753e-07) + 2.4761934264809493e-05
    c = c * h2 + (-0.0013888404392126607)
    c = c * h2 + 0.04166664079116777
    c = c * h2 + (-0.4999999955092854)
    c = c * h2 + 1.0
    s2 = s + s
    return s2 * c, 1.0 - s2 * s


def wave_kernel(
    n, jr, cols_per, now_hbm, prev_hbm, eps_hbm, tilt_hbm, azi_hbm, cou_hbm, cols_ref,
    buf0, buf1, sz0, sz1, dz0, dz1, eps, tilt, azi, cou, coef, zmat, pair, snap_send, sendbuf, halo,
    in_sems, prev_sem, own_sem, hs_sems, hr_sems, as_sems, ar_sems,
):
    width = eps.shape[0]
    ny = eps.shape[1]
    nz = eps.shape[2]
    half = width // 2
    chunks = ny // ROWS
    rows = pl.ds(PAD, ny)
    me = lax.axis_index("gx")
    has_low = me > 0
    has_high = me < n - 1
    bufs = (buf0, buf1)
    szs = (sz0, sz1)
    dzs = (dz0, dz1)
    group = width // GROUPS

    def group_copies(g):
        part = pl.ds(g * group, group)
        pairs = (
            (tilt_hbm.at[part], tilt.at[part]),
            (azi_hbm.at[part], azi.at[part]),
            (eps_hbm.at[part], eps.at[part]),
            (cou_hbm.at[part], cou.at[part]),
            (now_hbm.at[:, part], buf0.at[:, part, rows, :]),
        )
        return [
            pltpu.make_async_copy(src, dst, in_sems.at[g, k]) for k, (src, dst) in enumerate(pairs)
        ]

    for g in range(GROUPS):
        for copy in group_copies(g):
            copy.start()
    prev_copy = pltpu.make_async_copy(prev_hbm, buf1.at[:, :, rows, :], prev_sem)
    prev_copy.start()

    barrier = pltpu.get_barrier_semaphore()

    def greet(k, carry):
        pl.semaphore_signal(
            barrier, inc=1, device_id={"gx": lax.rem(me + k, n)},
            device_id_type=pl.DeviceIdType.MESH,
        )
        return carry

    lax.fori_loop(1, n, greet, 0)

    zero_rows = jnp.zeros((2, width, PAD, nz), F32)
    for ref in (buf0, buf1, dz0, dz1):
        ref[:, :, pl.ds(0, PAD), :] = zero_rows
        ref[:, :, pl.ds(PAD + ny, PAD), :] = zero_rows
    zero_ends = jnp.zeros((STEPS, 2, 2, PAD, nz), F32)
    halo[:, :, :, pl.ds(0, PAD), :] = zero_ends
    halo[:, :, :, pl.ds(PAD + ny, PAD), :] = zero_ends
    for side, has in ((0, has_low), (1, has_high)):
        @pl.when(jnp.logical_not(has))
        def _(side=side):
            halo[:, side, :, rows, :] = jnp.zeros((STEPS, 2, ny, nz), F32)

    r = lax.broadcasted_iota(jnp.int32, (nz, 2 * nz), 0)
    c = lax.broadcasted_iota(jnp.int32, (nz, 2 * nz), 1)
    second = c < nz
    cz = jnp.where(second, c, c - nz)
    zmat[...] = jnp.where(
        r == cz + 1, 1.0,
        jnp.where(r == cz - 1, jnp.where(second, 1.0, -1.0),
                  jnp.where((r == cz) & second, -2.0, 0.0)),
    ).astype(jnp.bfloat16)

    def halo_copy(step, side):
        if step == 0:
            src = now_hbm.at[:, 0 if side == 0 else width - 1]
        else:
            src = sendbuf.at[step - 1, side]
        return pltpu.make_async_remote_copy(
            src_ref=src,
            dst_ref=halo.at[step, 1 - side, :, rows, :],
            send_sem=hs_sems.at[step, side],
            recv_sem=hr_sems.at[step, 1 - side],
            device_id={"gx": me - 1 if side == 0 else me + 1},
            device_id_type=pl.DeviceIdType.MESH,
        )

    def halo_arrived(step, side):
        return pltpu.make_async_remote_copy(
            src_ref=sendbuf.at[0, side],
            dst_ref=halo.at[step, side, :, rows, :],
            send_sem=hs_sems.at[step, side],
            recv_sem=hr_sems.at[step, side],
            device_id={"gx": me - 1 if side == 0 else me + 1},
            device_id_type=pl.DeviceIdType.MESH,
        )

    def send_halo(step):
        for side, has in ((0, has_low), (1, has_high)):
            @pl.when(has)
            def _(side=side):
                halo_copy(step, side).start()

    def z_terms(p):
        return jnp.dot(p.astype(jnp.bfloat16), zmat[...], preferred_element_type=F32)

    def prepare(x, carry):
        found = z_terms(buf0[:, x, rows, :].reshape(2 * ny, nz))
        theta_s, theta_c = sin_cos(tilt[x].astype(F32))
        alpha_s, alpha_c = sin_cos(azi[x].astype(F32))
        speed = cou[x].astype(F32)
        e2 = eps[x].astype(F32) * 2.0
        scaled = speed * e2
        base = speed + scaled
        nx = theta_s * alpha_c
        nyy = theta_s * alpha_s
        sx = scaled * nx
        sy = scaled * nyy
        scz = scaled * theta_c
        mxx = base - sx * nx
        myy = base - sy * nyy
        coef[0, x] = mxx
        coef[1, x] = myy
        coef[2, x] = base - scz * theta_c
        coef[3, x] = -0.5 * (sx * nyy)
        coef[4, x] = -0.5 * (scz * nx)
        coef[5, x] = -0.5 * (scz * nyy)
        coef[6, x] = 2.0 - 2.0 * (mxx + myy)
        sz0[:, x, rows, :] = found[:, :nz].reshape(2, ny, nz)
        dz0[:, x, rows, :] = found[:, nz:].reshape(2, ny, nz)
        return carry

    for g in range(GROUPS):
        for copy in group_copies(g):
            copy.wait()
        lax.fori_loop(g * group, (g + 1) * group, prepare, 0)
        if g == 0:
            pl.semaphore_wait(barrier, n - 1)
            send_halo(0)
    prev_copy.wait()

    def combine(cs, p, old, px, sy, sz, yx, dzx, dzy):
        acc = cs[6] * p - old
        acc += cs[0] * px + cs[1] * sy
        acc += cs[2] * sz + cs[3] * yx
        acc += cs[4] * dzx + cs[5] * dzy
        return acc

    def edges(step):
        now, prv = bufs[step % 2], bufs[(step + 1) % 2]
        sz, dz = szs[step % 2], dzs[step % 2]
        for side, has in ((0, has_low), (1, has_high)):
            @pl.when(has)
            def _(side=side):
                halo_arrived(step, side).wait_recv()
        both = [halo[step, side, f, rows, :] for side in range(2) for f in range(2)]
        outer = jnp.dot(
            jnp.concatenate(both, axis=0).astype(jnp.bfloat16), zmat[:, nz:],
            preferred_element_type=F32,
        )
        for side in range(2):
            x = 0 if side == 0 else width - 1
            inner = 1 if side == 0 else width - 2
            for y in range(0, ny, EDGE):
                mid, up, dn = [pl.ds(PAD + y + d, EDGE) for d in (0, 1, -1)]
                cs = [coef[k, x, pl.ds(y, EDGE), :] for k in range(7)]
                for f in range(2):
                    a = halo[step, side, f, mid, :]
                    ya = halo[step, side, f, up, :] - halo[step, side, f, dn, :]
                    first = (side * 2 + f) * ny + y
                    za = outer[first : first + EDGE]
                    b = now[f, inner, mid, :]
                    yb = now[f, inner, up, :] - now[f, inner, dn, :]
                    zb = dz[f, inner, mid, :]
                    acc = combine(
                        cs, now[f, x, mid, :], prv[f, x, mid, :], a + b,
                        now[f, x, up, :] + now[f, x, dn, :], sz[f, x, mid, :],
                        yb - ya if side == 0 else ya - yb,
                        zb - za if side == 0 else za - zb,
                        dz[f, x, up, :] - dz[f, x, dn, :],
                    )
                    prv[f, x, mid, :] = acc
                    if step < STEPS - 1:
                        sendbuf[step, side, f, pl.ds(y, EDGE), :] = acc
        if step < STEPS - 1:
            send_halo(step + 1)

    def inside(step, base, emit):
        now, prv = bufs[step % 2], bufs[(step + 1) % 2]
        sz, dz = szs[step % 2], dzs[step % 2]
        mid, up, dn = [pl.ds(base + PAD + d, ROWS) for d in (0, 1, -1)]
        here = pl.ds(base, ROWS)
        p0, y0, d0, p1, y1, s1, d1 = [[None, None] for _ in range(7)]
        for f in range(2):
            p0[f] = now[f, 0, mid, :]
            y0[f] = now[f, 0, up, :] - now[f, 0, dn, :]
            d0[f] = dz[f, 0, mid, :]
            hi, lo = now[f, 1, up, :], now[f, 1, dn, :]
            p1[f], y1[f], s1[f], d1[f] = now[f, 1, mid, :], hi - lo, hi + lo, dz[f, 1, mid, :]
        for x in range(1, width - 1):
            cs = [coef[k, x, here, :] for k in range(7)]
            for f in range(2):
                hi, lo = now[f, x + 1, up, :], now[f, x + 1, dn, :]
                p2, y2, s2, d2 = now[f, x + 1, mid, :], hi - lo, hi + lo, dz[f, x + 1, mid, :]
                acc = combine(
                    cs, p1[f], prv[f, x, mid, :], p2 + p0[f], s1[f], sz[f, x, mid, :],
                    y2 - y0[f], d2 - d0[f], dz[f, x, up, :] - dz[f, x, dn, :],
                )
                emit(f, x, mid, acc)
                p0[f], y0[f], d0[f] = p1[f], y1[f], d1[f]
                p1[f], y1[f], s1[f], d1[f] = p2, y2, s2, d2

    def z_rows(step, base):
        prv, sz, dz = bufs[(step + 1) % 2], szs[(step + 1) % 2], dzs[(step + 1) % 2]
        at = pl.ds(base, ROWS)
        found = z_terms(jnp.concatenate([prv[f, x, at, :] for x in range(width) for f in range(2)], axis=0))
        for x in range(width):
            for f in range(2):
                first = (x * 2 + f) * ROWS
                sz[f, x, at, :] = found[first : first + ROWS, :nz]
                dz[f, x, at, :] = found[first : first + ROWS, nz:]

    for step in range(STEPS - 1):
        edges(step)

        def emit(f, x, mid, acc, prv=bufs[(step + 1) % 2]):
            prv[f, x, mid, :] = acc

        def advance(k, carry, step=step, emit=emit):
            base = pl.multiple_of(k * ROWS, ROWS)
            z_rows(step, base)
            inside(step, base, emit)
            return carry

        lax.fori_loop(0, chunks, advance, 0)
        z_rows(step, ny)

    edges(STEPS - 1)
    final = bufs[STEPS % 2]
    span = jr * half
    each = n // chunks

    def piece(target, source):
        start = pl.multiple_of(((target * cols_per) // nz) * half, half)
        return pltpu.make_async_remote_copy(
            src_ref=snap_send.at[:, pl.ds(start, span), :],
            dst_ref=cols_ref.at[source],
            send_sem=as_sems.at[target],
            recv_sem=ar_sems.at[source],
            device_id={"gx": target},
            device_id_type=pl.DeviceIdType.MESH,
        )

    start = pl.multiple_of(((me * cols_per) // nz) * half, half)
    own = pltpu.make_async_copy(snap_send.at[:, pl.ds(start, span), :], cols_ref.at[me], own_sem)

    def last(k, carry):
        away = (k + 1) // 2
        away = jnp.where(lax.rem(k, 2) == 1, chunks // 2 - away, chunks // 2 + away)
        block = lax.rem(me // each + away, chunks)
        base = pl.multiple_of(block * ROWS, ROWS)
        mid = pl.ds(base + PAD, ROWS)
        held = [final[f, 0, mid, :] for f in range(2)]

        def emit(f, x, mid, acc):
            if x % 2 == 0:
                held[f] = acc
            else:
                pair[f, pl.ds((x // 2) * ROWS, ROWS), :] = held[f] + acc

        inside(STEPS - 1, base, emit)
        for f in range(2):
            pair[f, pl.ds((half - 1) * ROWS, ROWS), :] = held[f] + final[f, width - 1, mid, :]
        for f in range(2):
            for j in range(ROWS // 2):
                even = pair[f, pl.ds(2 * j, half, stride=ROWS), :]
                odd = pair[f, pl.ds(2 * j + 1, half, stride=ROWS), :]
                at = pl.multiple_of((block * (ROWS // 2) + j) * half, half)
                snap_send[f, pl.ds(at, half), :] = ((even + odd) * 0.25).astype(SEND)

        def send(u, carry):
            target = block * each + u

            @pl.when(target != me)
            def _():
                piece(target, me).start()

            return carry

        lax.fori_loop(0, each, send, 0)
        return carry

    lax.fori_loop(0, chunks, last, 0)
    own.start()

    for step in range(STEPS):
        for side, has in ((0, has_low), (1, has_high)):
            @pl.when(has)
            def _(step=step, side=side):
                halo_copy(step, side).wait_send()

    def wait_piece(k, carry):
        piece(lax.rem(me + k, n), me).wait_send()
        piece(lax.rem(me + k, n), lax.rem(me + k, n)).wait_recv()
        return carry

    lax.fori_loop(1, n, wait_piece, 0)
    own.wait()


def image_kernel(
    cols_per, jr, offsets, tables_at, cols_ref, tab_ref, out_ref, lines, wide, prods
):
    n = cols_ref.shape[0]
    half = cols_ref.shape[2] // jr
    nz = cols_ref.shape[3]
    full = n * half
    step = pl.program_id(0)
    tables = tab_ref.shape[0]
    angles = tab_ref.shape[1]
    lags = tab_ref.shape[2]

    @pl.when(step == 0)
    def _():
        for f in range(2):
            for j in range(jr):
                for t in range(full // nz):
                    per = nz // half
                    block = cols_ref[pl.ds(t * per, per), f, pl.ds(j * half, half), :]
                    block = block.reshape(nz, nz).astype(F32)
                    lines[f, j, :, pl.ds(t * nz, nz)] = block.T.astype(SEND)
        lag = lax.broadcasted_iota(jnp.int32, (lags, lags * 8), 0)
        col = lax.broadcasted_iota(jnp.int32, (lags, lags * 8), 1)
        spread = jnp.where(col // 8 == lag, 1.0, 0.0).astype(jnp.bfloat16)
        flat = tab_ref[...].reshape(tables * angles, lags)
        wide[...] = jnp.dot(flat, spread, preferred_element_type=F32).astype(jnp.bfloat16)

    me = lax.axis_index("gx")
    z0 = lax.rem(me * cols_per, nz)
    lane = lax.broadcasted_iota(jnp.int32, (16, nz), 1)
    tiles = full // nz
    ta = tables * angles
    sub = lax.broadcasted_iota(jnp.int32, (8, ta), 0)
    row_c = lax.rem(lax.broadcasted_iota(jnp.int32, (angles * 8, lags * 8), 0), 8)
    col_c = lax.rem(lax.broadcasted_iota(jnp.int32, (angles * 8, lags * 8), 1), 8)
    diagonal = row_c == col_c
    lane_ta = lax.broadcasted_iota(jnp.int32, (angles, 8, ta), 2)
    row_a = lax.broadcasted_iota(jnp.int32, (angles, 8, ta), 0)
    weights = []
    for q in range(2):
        row0 = z0 + step * 16 + q * 8
        chosen = jnp.zeros((8, ta), jnp.int32)
        for c in range(8):
            chosen = jnp.where(sub == c, tables_at[row0 + c], chosen)
        wanted = (chosen * angles)[None] + row_a
        pick = jnp.where(lane_ta == wanted, 1.0, 0.0).reshape(angles * 8, ta)
        dense = jnp.dot(pick.astype(jnp.bfloat16), wide[...], preferred_element_type=F32)
        weights.append(jnp.where(diagonal, dense, 0.0).astype(jnp.bfloat16))

    def moved(parts, d):
        if d == 0:
            return [part.astype(F32) for part in parts]
        turned = [pltpu.roll(part, d % nz, axis=1).astype(F32) for part in parts]
        zero = jnp.zeros((16, nz), F32)
        if d > 0:
            return [
                jnp.where(lane >= d, turned[t], turned[t - 1] if t else zero)
                for t in range(tiles)
            ]
        return [
            jnp.where(lane < nz + d, turned[t], turned[t + 1] if t + 1 < tiles else zero)
            for t in range(tiles)
        ]

    for j in range(jr):
        results = []
        row0 = pl.multiple_of(z0 + step * 16, 16)
        source = [lines[0, j, pl.ds(row0, 16), pl.ds(t * nz, nz)] for t in range(tiles)]
        receiver = [lines[1, j, pl.ds(row0, 16), pl.ds(t * nz, nz)] for t in range(tiles)]
        for d in range(-LAG_REACH, LAG_REACH):
            left, right = moved(source, d), moved(receiver, -d)
            for t in range(tiles):
                product = left[t] * right[t]
                for q in range(2):
                    prods[j * 2 + q, d + LAG_REACH, :, pl.ds(t * nz, nz)] = product[8 * q : 8 * q + 8]
        for q in range(2):
            slot = j * 2 + q
            lagged = jnp.concatenate(
                [prods[slot, offsets[h] + LAG_REACH] for h in range(lags)], axis=0
            ).astype(jnp.bfloat16)
            total = jnp.dot(weights[q], lagged, preferred_element_type=F32)
            results.append(total.reshape(angles, 8, full))
        both = jnp.concatenate(results, axis=1)
        out_ref[:, j] = both.astype(jnp.bfloat16)


def local(
    waves_now, waves_prev, epsilon, tilt, azimuth, courant, lag_offsets, table_index, lag_tables
):
    n = lax.axis_size("gx")
    width, ny, nz = epsilon.shape
    half = width // 2
    columns = (ny // 2) * nz
    cols_per = columns // n
    jr = max(1, cols_per // nz)
    full = n * half
    plane = (2, width, ny + 2 * PAD, nz)
    dma = pltpu.SemaphoreType.DMA
    cols = pl.pallas_call(
        functools.partial(wave_kernel, n, jr, cols_per),
        out_shape=jax.ShapeDtypeStruct((n, 2, jr * half, nz), SEND),
        in_specs=[pl.BlockSpec(memory_space=pltpu.HBM)] * 6,
        out_specs=pl.BlockSpec(memory_space=pltpu.VMEM),
        scratch_shapes=[
            pltpu.VMEM(plane, F32),
            pltpu.VMEM(plane, F32),
            pltpu.VMEM(plane, F32),
            pltpu.VMEM(plane, F32),
            pltpu.VMEM(plane, F32),
            pltpu.VMEM(plane, F32),
            pltpu.VMEM((width, ny, nz), epsilon.dtype),
            pltpu.VMEM((width, ny, nz), tilt.dtype),
            pltpu.VMEM((width, ny, nz), azimuth.dtype),
            pltpu.VMEM((width, ny, nz), courant.dtype),
            pltpu.VMEM((7, width, ny, nz), F32),
            pltpu.VMEM((nz, 2 * nz), jnp.bfloat16),
            pltpu.VMEM((2, half * ROWS, nz), F32),
            pltpu.VMEM((2, (ny // 2) * half, nz), SEND),
            pltpu.VMEM((STEPS - 1, 2, 2, ny, nz), F32),
            pltpu.VMEM((STEPS, 2, 2, ny + 2 * PAD, nz), F32),
            dma((GROUPS, 5)),
            dma,
            dma,
            dma((STEPS, 2)),
            dma((STEPS, 2)),
            dma((n,)),
            dma((n,)),
        ],
        compiler_params=pltpu.CompilerParams(
            collective_id=0, has_side_effects=True, vmem_limit_bytes=60 << 20
        ),
        name="waves",
    )(waves_now, waves_prev, epsilon, tilt, azimuth, courant)

    angles, lags = lag_tables.shape[1:]
    tables = lag_tables.shape[0]
    cz = min(cols_per, nz)
    image = pl.pallas_call(
        functools.partial(image_kernel, cols_per, jr),
        grid=(cz // 16,),
        out_shape=jax.ShapeDtypeStruct((angles, jr, cz, full), jnp.bfloat16),
        in_specs=[
            pl.BlockSpec(memory_space=pltpu.SMEM),
            pl.BlockSpec(memory_space=pltpu.SMEM),
            pl.BlockSpec(memory_space=pltpu.VMEM),
            pl.BlockSpec(memory_space=pltpu.VMEM),
        ],
        out_specs=pl.BlockSpec((angles, jr, 16, full), lambda g: (0, 0, g, 0)),
        scratch_shapes=[
            pltpu.VMEM((2, jr, nz, full), SEND),
            pltpu.VMEM((tables * angles, lags * 8), jnp.bfloat16),
            pltpu.VMEM((jr * 2, 2 * LAG_REACH, 8, full), F32),
        ],
        compiler_params=pltpu.CompilerParams(vmem_limit_bytes=60 << 20),
        name="image",
    )(lag_offsets, table_index, cols, lag_tables)
    return image.reshape(angles, cols_per, full)


def solution(mesh):
    wave = P(None, ("shot", "gx"), None, None)
    cell = P("gx", None, None)
    return jax.shard_map(
        local,
        mesh=mesh,
        in_specs=(wave, wave, cell, cell, cell, cell, P(), P(), P()),
        out_specs=P(None, ("shot", "gx"), None),
        check_vma=False,
    )
```

time: 41 us -> 37.4 us (0.912)
  Pallas kernels: 40.8 us -> 37.2 us
    pallas_call x1, Pallas kernels: 33.2 us -> 29.6 us  [local(): pl.pallas_call(functools.partial(wave_kernel, n, jr, cols_per), out_shape...]
where the time goes in v1:
time: 37.4 us; the launch traced here: 37.2 us
  Pallas kernels  37.2 us (99%)
    pallas_call x1, Pallas kernels, local(): pl.pallas_call(functools.partial(wave_kernel, n, jr, cols_per), out_shape...  29.6 us
    pallas_call x1, Pallas kernels, local(): pl.pallas_call(functools.partial(image_kernel, cols_per, jr), grid=(cz //...  7.66 us

profile of v1, /device:TPU:0, one launch (start us, length us, event | category | flops | bytes accessed | tf_op | source)
XLA Modules:
  0.0 37.2 jit_solution(14612774764675299030)
XLA Ops:
  0.0 29.6 %waves.1.cols_ref = bf16[16,2,32,128]{3,2,1,0:T(8,128)(2,1)} custom-call(f32[2,32,64,128]{3,2,1,0:T(8,128)} %now_hbm.1, f32[2,32,64,128]{3,2,1,0:T(8,128)} %prev_hbm.1, bf16[32,64,128]{2,1,0:T(8,128)(2,1)} %eps_hbm.1, bf16[32,64,128]{2,1,0:T(8,128)(2,1)} %tilt_hbm.1, bf16[32,64,128]{2,1,0:T(8,128)(2,1)} %azi_hbm.1, bf16[32,64,128]{2,1,0:T(8,128)(2,1)} %cou_hbm.1), custom_call_target="tpu_custom_call" | custom-call | tf_op jit(solution)/shard_map/waves/pallas_call | solution.py:441
  29.6 7.7 %image.1 = bf16[32,2,128,256]{3,2,1,0:T(8,128)(2,1)} custom-call(s32[32]{0:T(128)} %offsets.1, s32[128]{0:T(128)} %tables_at.1, bf16[16,2,32,128]{3,2,1,0:T(8,128)(2,1)} %waves.1.cols_ref, bf16[4,32,32]{2,1,0:T(8,128)(2,1)} %tab_ref.1), custom_call_target="tpu_custom_call" | custom-call | tf_op jit(solution)/shard_map/image/pallas_call | solution.py:480

commit v2 on v1

--- a/solution.py
+++ b/solution.py
@@ -8,8 +8,10 @@
 
 STEPS = 4
 LAG_REACH = 16
-PAD = 8
+PAD = 16
 ROWS = 8
+DEPTH = 32
+TALL = 16
 EDGE = 32
 GROUPS = 4
 F32 = jnp.float32
@@ -17,19 +19,18 @@
 
 
 def sin_cos(x):
-    h = x * 0.5
-    h2 = h * h
-    s = h2 * 2.609020676498479e-06 + (-0.00019811149207883466)
-    s = s * h2 + 0.008333088613525165
-    s = s * h2 + (-0.16666660477455342)
-    s = s * h2 * h + h
-    c = h2 * (-2.607799327383753e-07) + 2.4761934264809493e-05
-    c = c * h2 + (-0.0013888404392126607)
-    c = c * h2 + 0.04166664079116777
-    c = c * h2 + (-0.4999999955092854)
-    c = c * h2 + 1.0
-    s2 = s + s
-    return s2 * c, 1.0 - s2 * s
+    u = x * x
+    s = u * 7.206469580499954e-09 - 2.1888434293738905e-06
+    s = s * u + 0.00036827396667825314
+    s = s * u - 0.029462771608356236
+    s = s * u + 0.7071067811865476
+    s = s * x
+    c = u * -3.6015480241538463e-10 + 1.3679165339017438e-07
+    c = c * u - 3.0689327892292986e-05
+    c = c * u + 0.003682845531587343
+    c = c * u - 0.17677669370892954
+    c = c * u + 1.4142135623730951
+    return s * c, 1.0 - s * s
 
 
 def wave_kernel(
@@ -217,11 +218,11 @@
         if step < STEPS - 1:
             send_halo(step + 1)
 
-    def inside(step, base, emit):
+    def inside(step, base, emit, tall):
         now, prv = bufs[step % 2], bufs[(step + 1) % 2]
         sz, dz = szs[step % 2], dzs[step % 2]
-        mid, up, dn = [pl.ds(base + PAD + d, ROWS) for d in (0, 1, -1)]
-        here = pl.ds(base, ROWS)
+        mid, up, dn = [pl.ds(base + PAD + d, tall) for d in (0, 1, -1)]
+        here = pl.ds(base, tall)
         p0, y0, d0, p1, y1, s1, d1 = [[None, None] for _ in range(7)]
         for f in range(2):
             p0[f] = now[f, 0, mid, :]
@@ -244,13 +245,13 @@
 
     def z_rows(step, base):
         prv, sz, dz = bufs[(step + 1) % 2], szs[(step + 1) % 2], dzs[(step + 1) % 2]
-        at = pl.ds(base, ROWS)
+        at = pl.ds(base, TALL)
         found = z_terms(jnp.concatenate([prv[f, x, at, :] for x in range(width) for f in range(2)], axis=0))
         for x in range(width):
             for f in range(2):
-                first = (x * 2 + f) * ROWS
-                sz[f, x, at, :] = found[first : first + ROWS, :nz]
-                dz[f, x, at, :] = found[first : first + ROWS, nz:]
+                first = (x * 2 + f) * TALL
+                sz[f, x, at, :] = found[first : first + TALL, :nz]
+                dz[f, x, at, :] = found[first : first + TALL, nz:]
 
     for step in range(STEPS - 1):
         edges(step)
@@ -259,13 +260,13 @@
             prv[f, x, mid, :] = acc
 
         def advance(k, carry, step=step, emit=emit):
-            base = pl.multiple_of(k * ROWS, ROWS)
-            z_rows(step, base)
-            inside(step, base, emit)
+            base = pl.multiple_of(k * TALL, TALL)
+            z_rows(step, base + PAD - TALL)
+            inside(step, base, emit, TALL)
             return carry
 
-        lax.fori_loop(0, chunks, advance, 0)
-        z_rows(step, ny)
+        lax.fori_loop(0, ny // TALL, advance, 0)
+        z_rows(step, PAD + ny - TALL)
 
     edges(STEPS - 1)
     final = bufs[STEPS % 2]
@@ -287,9 +288,14 @@
     own = pltpu.make_async_copy(snap_send.at[:, pl.ds(start, span), :], cols_ref.at[me], own_sem)
 
     def last(k, carry):
-        away = (k + 1) // 2
-        away = jnp.where(lax.rem(k, 2) == 1, chunks // 2 - away, chunks // 2 + away)
-        block = lax.rem(me // each + away, chunks)
+        mine = me // each
+        low = 2 * mine < chunks
+        near = jnp.where(low, mine, chunks - 1 - mine)
+        lead = chunks - 1 - 2 * near
+        rest = jnp.maximum(k - lead, 0)
+        pick = jnp.where(lax.rem(rest, 2) == 0, 2 * near - rest // 2, rest // 2)
+        pick = jnp.where(k < lead, chunks - 1 - k, pick)
+        block = jnp.where(low, pick, chunks - 1 - pick)
         base = pl.multiple_of(block * ROWS, ROWS)
         mid = pl.ds(base + PAD, ROWS)
         held = [final[f, 0, mid, :] for f in range(2)]
@@ -300,7 +306,7 @@
             else:
                 pair[f, pl.ds((x // 2) * ROWS, ROWS), :] = held[f] + acc
 
-        inside(STEPS - 1, base, emit)
+        inside(STEPS - 1, base, emit, ROWS)
         for f in range(2):
             pair[f, pl.ds((half - 1) * ROWS, ROWS), :] = held[f] + final[f, width - 1, mid, :]
         for f in range(2):
@@ -341,13 +347,14 @@
 
 
 def image_kernel(
-    cols_per, jr, offsets, tables_at, cols_ref, tab_ref, out_ref, lines, wide, prods
+    cols_per, jr, offsets, tables_at, cols_ref, tab_ref, out_ref, lines, wide, keep, prods
 ):
     n = cols_ref.shape[0]
     half = cols_ref.shape[2] // jr
     nz = cols_ref.shape[3]
     full = n * half
     step = pl.program_id(0)
+    blocks = pl.num_programs(0) - 1
     tables = tab_ref.shape[0]
     angles = tab_ref.shape[1]
     lags = tab_ref.shape[2]
@@ -366,34 +373,48 @@
         spread = jnp.where(col // 8 == lag, 1.0, 0.0).astype(jnp.bfloat16)
         flat = tab_ref[...].reshape(tables * angles, lags)
         wide[...] = jnp.dot(flat, spread, preferred_element_type=F32).astype(jnp.bfloat16)
+        row_c = lax.rem(lax.broadcasted_iota(jnp.int32, (angles * 8, lags * 8), 0), 8)
+        col_c = lax.rem(lax.broadcasted_iota(jnp.int32, (angles * 8, lags * 8), 1), 8)
+        keep[...] = jnp.where(row_c == col_c, 1.0, 0.0).astype(jnp.bfloat16)
 
     me = lax.axis_index("gx")
     z0 = lax.rem(me * cols_per, nz)
-    lane = lax.broadcasted_iota(jnp.int32, (16, nz), 1)
     tiles = full // nz
     ta = tables * angles
+    slot = lax.rem(step, 2)
+    before = 1 - slot
+
     sub = lax.broadcasted_iota(jnp.int32, (8, ta), 0)
-    row_c = lax.rem(lax.broadcasted_iota(jnp.int32, (angles * 8, lags * 8), 0), 8)
-    col_c = lax.rem(lax.broadcasted_iota(jnp.int32, (angles * 8, lags * 8), 1), 8)
-    diagonal = row_c == col_c
     lane_ta = lax.broadcasted_iota(jnp.int32, (angles, 8, ta), 2)
     row_a = lax.broadcasted_iota(jnp.int32, (angles, 8, ta), 0)
     weights = []
-    for q in range(2):
-        row0 = z0 + step * 16 + q * 8
+    for q in range(DEPTH // 8):
+        row0 = z0 + jnp.maximum(step - 1, 0) * DEPTH + q * 8
         chosen = jnp.zeros((8, ta), jnp.int32)
         for c in range(8):
             chosen = jnp.where(sub == c, tables_at[row0 + c], chosen)
         wanted = (chosen * angles)[None] + row_a
         pick = jnp.where(lane_ta == wanted, 1.0, 0.0).reshape(angles * 8, ta)
         dense = jnp.dot(pick.astype(jnp.bfloat16), wide[...], preferred_element_type=F32)
-        weights.append(jnp.where(diagonal, dense, 0.0).astype(jnp.bfloat16))
+        weights.append(dense.astype(jnp.bfloat16) * keep[...])
+
+    for j in range(jr):
+        results = []
+        for q in range(DEPTH // 8):
+            lagged = jnp.concatenate(
+                [prods[before, j * (DEPTH // 8) + q, offsets[h] + LAG_REACH] for h in range(lags)], axis=0
+            ).astype(jnp.bfloat16)
+            total = jnp.dot(weights[q], lagged, preferred_element_type=F32)
+            results.append(total.reshape(angles, 8, full))
+        out_ref[:, j] = jnp.concatenate(results, axis=1).astype(jnp.bfloat16)
+
+    lane = lax.broadcasted_iota(jnp.int16, (DEPTH, nz), 1)
+    zero = jnp.zeros((DEPTH, nz), SEND)
 
     def moved(parts, d):
         if d == 0:
-            return [part.astype(F32) for part in parts]
-        turned = [pltpu.roll(part, d % nz, axis=1).astype(F32) for part in parts]
-        zero = jnp.zeros((16, nz), F32)
+            return parts
+        turned = [pltpu.roll(part, d % nz, axis=1) for part in parts]
         if d > 0:
             return [
                 jnp.where(lane >= d, turned[t], turned[t - 1] if t else zero)
@@ -404,26 +425,16 @@
             for t in range(tiles)
         ]
 
+    row0 = pl.multiple_of(z0 + jnp.minimum(step, blocks - 1) * DEPTH, DEPTH)
     for j in range(jr):
-        results = []
-        row0 = pl.multiple_of(z0 + step * 16, 16)
-        source = [lines[0, j, pl.ds(row0, 16), pl.ds(t * nz, nz)] for t in range(tiles)]
-        receiver = [lines[1, j, pl.ds(row0, 16), pl.ds(t * nz, nz)] for t in range(tiles)]
+        source = [lines[0, j, pl.ds(row0, DEPTH), pl.ds(t * nz, nz)] for t in range(tiles)]
+        receiver = [lines[1, j, pl.ds(row0, DEPTH), pl.ds(t * nz, nz)] for t in range(tiles)]
         for d in range(-LAG_REACH, LAG_REACH):
             left, right = moved(source, d), moved(receiver, -d)
             for t in range(tiles):
-                product = left[t] * right[t]
-                for q in range(2):
-                    prods[j * 2 + q, d + LAG_REACH, :, pl.ds(t * nz, nz)] = product[8 * q : 8 * q + 8]
-        for q in range(2):
-            slot = j * 2 + q
-            lagged = jnp.concatenate(
-                [prods[slot, offsets[h] + LAG_REACH] for h in range(lags)], axis=0
-            ).astype(jnp.bfloat16)
-            total = jnp.dot(weights[q], lagged, preferred_element_type=F32)
-            results.append(total.reshape(angles, 8, full))
-        both = jnp.concatenate(results, axis=1)
-        out_ref[:, j] = both.astype(jnp.bfloat16)
+                product = (left[t] * right[t]).astype(F32)
+                for q in range(DEPTH // 8):
+                    prods[slot, j * (DEPTH // 8) + q, d + LAG_REACH, :, pl.ds(t * nz, nz)] = product[8 * q : 8 * q + 8]
 
 
 def local(
@@ -442,7 +453,7 @@
         functools.partial(wave_kernel, n, jr, cols_per),
         out_shape=jax.ShapeDtypeStruct((n, 2, jr * half, nz), SEND),
         in_specs=[pl.BlockSpec(memory_space=pltpu.HBM)] * 6,
-        out_specs=pl.BlockSpec(memory_space=pltpu.VMEM),
+        out_specs=pl.BlockSpec(memory_space=pl.ANY),
         scratch_shapes=[
             pltpu.VMEM(plane, F32),
             pltpu.VMEM(plane, F32),
@@ -479,7 +490,7 @@
     cz = min(cols_per, nz)
     image = pl.pallas_call(
         functools.partial(image_kernel, cols_per, jr),
-        grid=(cz // 16,),
+        grid=(cz // DEPTH + 1,),
         out_shape=jax.ShapeDtypeStruct((angles, jr, cz, full), jnp.bfloat16),
         in_specs=[
             pl.BlockSpec(memory_space=pltpu.SMEM),
@@ -487,11 +498,12 @@
             pl.BlockSpec(memory_space=pltpu.VMEM),
             pl.BlockSpec(memory_space=pltpu.VMEM),
         ],
-        out_specs=pl.BlockSpec((angles, jr, 16, full), lambda g: (0, 0, g, 0)),
+        out_specs=pl.BlockSpec((angles, jr, DEPTH, full), lambda g: (0, 0, jnp.maximum(g - 1, 0), 0)),
         scratch_shapes=[
             pltpu.VMEM((2, jr, nz, full), SEND),
             pltpu.VMEM((tables * angles, lags * 8), jnp.bfloat16),
-            pltpu.VMEM((jr * 2, 2 * LAG_REACH, 8, full), F32),
+            pltpu.VMEM((angles * 8, lags * 8), jnp.bfloat16),
+            pltpu.VMEM((2, jr * (DEPTH // 8), 2 * LAG_REACH, 8, full), F32),
         ],
         compiler_params=pltpu.CompilerParams(vmem_limit_bytes=60 << 20),
         name="image",

time: 37.4 us -> 34.9 us (0.933); the launches traced: 37.2 us -> 34.3 us
  Pallas kernels: 37.2 us -> 34.3 us
    pallas_call x1, Pallas kernels: 29.6 us -> 27.9 us  [local(): pl.pallas_call(functools.partial(wave_kernel, n, jr, cols_per), out_shape...]
    pallas_call x1, Pallas kernels: 7.66 us -> 6.47 us  [local(): pl.pallas_call(functools.partial(image_kernel, cols_per, jr), grid=(cz //...]
where the time goes in v2:
time: 34.9 us; the launch traced here: 34.3 us
  Pallas kernels  34.3 us (98%)
    pallas_call x1, Pallas kernels, local(): pl.pallas_call(functools.partial(wave_kernel, n, jr, cols_per), out_shape...  27.9 us
    pallas_call x1, Pallas kernels, local(): pl.pallas_call(functools.partial(image_kernel, cols_per, jr), grid=(cz //...  6.47 us

profile of v2, /device:TPU:0, one launch (start us, length us, event | category | flops | bytes accessed | tf_op | source)
XLA Modules:
  0.0 34.3 jit_solution(1243289916423423146)
XLA Ops:
  0.0 27.9 %waves.1.cols_ref = bf16[16,2,32,128]{3,2,1,0:T(8,128)(2,1)} custom-call(f32[2,32,64,128]{3,2,1,0:T(8,128)} %now_hbm.1, f32[2,32,64,128]{3,2,1,0:T(8,128)} %prev_hbm.1, bf16[32,64,128]{2,1,0:T(8,128)(2,1)} %eps_hbm.1, bf16[32,64,128]{2,1,0:T(8,128)(2,1)} %tilt_hbm.1, bf16[32,64,128]{2,1,0:T(8,128)(2,1)} %azi_hbm.1, bf16[32,64,128]{2,1,0:T(8,128)(2,1)} %cou_hbm.1), custom_call_target="tpu_custom_call" | custom-call | tf_op jit(solution)/shard_map/waves/pallas_call | solution.py:452
  27.9 6.5 %image.1 = bf16[32,2,128,256]{3,2,1,0:T(8,128)(2,1)} custom-call(s32[32]{0:T(128)} %offsets.1, s32[128]{0:T(128)} %tables_at.1, bf16[16,2,32,128]{3,2,1,0:T(8,128)(2,1)} %waves.1.cols_ref, bf16[4,32,32]{2,1,0:T(8,128)(2,1)} %tab_ref.1), custom_call_target="tpu_custom_call" | custom-call | tf_op jit(solution)/shard_map/image/pallas_call | solution.py:491

commit v3 on v2

--- a/solution.py
+++ b/solution.py
@@ -166,7 +166,7 @@
     for g in range(GROUPS):
         for copy in group_copies(g):
             copy.wait()
-        lax.fori_loop(g * group, (g + 1) * group, prepare, 0)
+        lax.fori_loop(g * group, (g + 1) * group, prepare, 0, unroll=4)
         if g == 0:
             pl.semaphore_wait(barrier, n - 1)
             send_halo(0)
@@ -347,14 +347,13 @@
 
 
 def image_kernel(
-    cols_per, jr, offsets, tables_at, cols_ref, tab_ref, out_ref, lines, wide, keep, prods
+    cols_per, jr, offsets, tables_at, cols_ref, tab_ref, out_ref, lines, wide, keep, *prods
 ):
     n = cols_ref.shape[0]
     half = cols_ref.shape[2] // jr
     nz = cols_ref.shape[3]
     full = n * half
     step = pl.program_id(0)
-    blocks = pl.num_programs(0) - 1
     tables = tab_ref.shape[0]
     angles = tab_ref.shape[1]
     lags = tab_ref.shape[2]
@@ -381,15 +380,13 @@
     z0 = lax.rem(me * cols_per, nz)
     tiles = full // nz
     ta = tables * angles
-    slot = lax.rem(step, 2)
-    before = 1 - slot
 
     sub = lax.broadcasted_iota(jnp.int32, (8, ta), 0)
     lane_ta = lax.broadcasted_iota(jnp.int32, (angles, 8, ta), 2)
     row_a = lax.broadcasted_iota(jnp.int32, (angles, 8, ta), 0)
     weights = []
     for q in range(DEPTH // 8):
-        row0 = z0 + jnp.maximum(step - 1, 0) * DEPTH + q * 8
+        row0 = z0 + step * DEPTH + q * 8
         chosen = jnp.zeros((8, ta), jnp.int32)
         for c in range(8):
             chosen = jnp.where(sub == c, tables_at[row0 + c], chosen)
@@ -397,16 +394,6 @@
         pick = jnp.where(lane_ta == wanted, 1.0, 0.0).reshape(angles * 8, ta)
         dense = jnp.dot(pick.astype(jnp.bfloat16), wide[...], preferred_element_type=F32)
         weights.append(dense.astype(jnp.bfloat16) * keep[...])
-
-    for j in range(jr):
-        results = []
-        for q in range(DEPTH // 8):
-            lagged = jnp.concatenate(
-                [prods[before, j * (DEPTH // 8) + q, offsets[h] + LAG_REACH] for h in range(lags)], axis=0
-            ).astype(jnp.bfloat16)
-            total = jnp.dot(weights[q], lagged, preferred_element_type=F32)
-            results.append(total.reshape(angles, 8, full))
-        out_ref[:, j] = jnp.concatenate(results, axis=1).astype(jnp.bfloat16)
 
     lane = lax.broadcasted_iota(jnp.int16, (DEPTH, nz), 1)
     zero = jnp.zeros((DEPTH, nz), SEND)
@@ -425,7 +412,7 @@
             for t in range(tiles)
         ]
 
-    row0 = pl.multiple_of(z0 + jnp.minimum(step, blocks - 1) * DEPTH, DEPTH)
+    row0 = pl.multiple_of(z0 + step * DEPTH, DEPTH)
     for j in range(jr):
         source = [lines[0, j, pl.ds(row0, DEPTH), pl.ds(t * nz, nz)] for t in range(tiles)]
         receiver = [lines[1, j, pl.ds(row0, DEPTH), pl.ds(t * nz, nz)] for t in range(tiles)]
@@ -434,7 +421,17 @@
             for t in range(tiles):
                 product = (left[t] * right[t]).astype(F32)
                 for q in range(DEPTH // 8):
-                    prods[slot, j * (DEPTH // 8) + q, d + LAG_REACH, :, pl.ds(t * nz, nz)] = product[8 * q : 8 * q + 8]
+                    prods[j * (DEPTH // 8) + q][d + LAG_REACH, :, pl.ds(t * nz, nz)] = product[8 * q : 8 * q + 8]
+
+    for j in range(jr):
+        results = []
+        for q in range(DEPTH // 8):
+            lagged = jnp.concatenate(
+                [prods[j * (DEPTH // 8) + q][offsets[h] + LAG_REACH] for h in range(lags)], axis=0
+            ).astype(jnp.bfloat16)
+            total = jnp.dot(weights[q], lagged, preferred_element_type=F32)
+            results.append(total.reshape(angles, 8, full))
+        out_ref[:, j] = jnp.concatenate(results, axis=1).astype(jnp.bfloat16)
 
 
 def local(
@@ -490,7 +487,7 @@
     cz = min(cols_per, nz)
     image = pl.pallas_call(
         functools.partial(image_kernel, cols_per, jr),
-        grid=(cz // DEPTH + 1,),
+        grid=(cz // DEPTH,),
         out_shape=jax.ShapeDtypeStruct((angles, jr, cz, full), jnp.bfloat16),
         in_specs=[
             pl.BlockSpec(memory_space=pltpu.SMEM),
@@ -498,13 +495,12 @@
             pl.BlockSpec(memory_space=pltpu.VMEM),
             pl.BlockSpec(memory_space=pltpu.VMEM),
         ],
-        out_specs=pl.BlockSpec((angles, jr, DEPTH, full), lambda g: (0, 0, jnp.maximum(g - 1, 0), 0)),
+        out_specs=pl.BlockSpec((angles, jr, DEPTH, full), lambda g: (0, 0, g, 0)),
         scratch_shapes=[
             pltpu.VMEM((2, jr, nz, full), SEND),
             pltpu.VMEM((tables * angles, lags * 8), jnp.bfloat16),
             pltpu.VMEM((angles * 8, lags * 8), jnp.bfloat16),
-            pltpu.VMEM((2, jr * (DEPTH // 8), 2 * LAG_REACH, 8, full), F32),
-        ],
+        ] + [pltpu.VMEM((2 * LAG_REACH, 8, full), F32)] * (jr * (DEPTH // 8)),
         compiler_params=pltpu.CompilerParams(vmem_limit_bytes=60 << 20),
         name="image",
     )(lag_offsets, table_index, cols, lag_tables)

time: 34.9 us -> 33.1 us (0.948); the launches traced: 34.3 us -> 32.9 us
  Pallas kernels: 34.3 us -> 32.9 us
    pallas_call x1, Pallas kernels: 27.9 us -> 26.7 us  [local(): pl.pallas_call(functools.partial(wave_kernel, n, jr, cols_per), out_shape...]
where the time goes in v3:
time: 33.1 us; the launch traced here: 32.9 us
  Pallas kernels  32.9 us (99%)
    pallas_call x1, Pallas kernels, local(): pl.pallas_call(functools.partial(wave_kernel, n, jr, cols_per), out_shape...  26.7 us
    pallas_call x1, Pallas kernels, local(): pl.pallas_call(functools.partial(image_kernel, cols_per, jr), grid=(cz //...  6.23 us

profile of v3, /device:TPU:0, one launch (start us, length us, event | category | flops | bytes accessed | tf_op | source)
XLA Modules:
  0.0 32.9 jit_solution(6679657285955024143)
XLA Ops:
  0.0 26.7 %waves.1.cols_ref = bf16[16,2,32,128]{3,2,1,0:T(8,128)(2,1)} custom-call(f32[2,32,64,128]{3,2,1,0:T(8,128)} %now_hbm.1, f32[2,32,64,128]{3,2,1,0:T(8,128)} %prev_hbm.1, bf16[32,64,128]{2,1,0:T(8,128)(2,1)} %eps_hbm.1, bf16[32,64,128]{2,1,0:T(8,128)(2,1)} %tilt_hbm.1, bf16[32,64,128]{2,1,0:T(8,128)(2,1)} %azi_hbm.1, bf16[32,64,128]{2,1,0:T(8,128)(2,1)} %cou_hbm.1), custom_call_target="tpu_custom_call" | custom-call | tf_op jit(solution)/shard_map/waves/pallas_call | solution.py:449
  26.7 6.2 %image.1 = bf16[32,2,128,256]{3,2,1,0:T(8,128)(2,1)} custom-call(s32[32]{0:T(128)} %offsets.1, s32[128]{0:T(128)} %tables_at.1, bf16[16,2,32,128]{3,2,1,0:T(8,128)(2,1)} %waves.1.cols_ref, bf16[4,32,32]{2,1,0:T(8,128)(2,1)} %tab_ref.1), custom_call_target="tpu_custom_call" | custom-call | tf_op jit(solution)/shard_map/image/pallas_call | solution.py:488

commit v4 on v3

--- a/solution.py
+++ b/solution.py
@@ -35,7 +35,7 @@
 
 def wave_kernel(
     n, jr, cols_per, now_hbm, prev_hbm, eps_hbm, tilt_hbm, azi_hbm, cou_hbm, cols_ref,
-    buf0, buf1, sz0, sz1, dz0, dz1, eps, tilt, azi, cou, coef, zmat, pair, snap_send, sendbuf, halo,
+    buf0, buf1, sz0, sz1, dz0, dz1, eps, tilt, azi, cou, coef, zmat, pair, snap_send, sendbuf, halo, arrived,
     in_sems, prev_sem, own_sem, hs_sems, hr_sems, as_sems, ar_sems,
 ):
     width = eps.shape[0]
@@ -86,13 +86,14 @@
     for ref in (buf0, buf1, dz0, dz1):
         ref[:, :, pl.ds(0, PAD), :] = zero_rows
         ref[:, :, pl.ds(PAD + ny, PAD), :] = zero_rows
-    zero_ends = jnp.zeros((STEPS, 2, 2, PAD, nz), F32)
-    halo[:, :, :, pl.ds(0, PAD), :] = zero_ends
-    halo[:, :, :, pl.ds(PAD + ny, PAD), :] = zero_ends
+    zero_ends = jnp.zeros((2, 2, PAD, nz), F32)
+    halo[:, :, pl.ds(0, PAD), :] = zero_ends
+    halo[:, :, pl.ds(PAD + ny, PAD), :] = zero_ends
     for side, has in ((0, has_low), (1, has_high)):
         @pl.when(jnp.logical_not(has))
         def _(side=side):
-            halo[:, side, :, rows, :] = jnp.zeros((STEPS, 2, ny, nz), F32)
+            halo[side, :, rows, :] = jnp.zeros((2, ny, nz), F32)
+            arrived[:, side] = jnp.zeros((STEPS - 1, 2, ny, nz), SEND)
 
     r = lax.broadcasted_iota(jnp.int32, (nz, 2 * nz), 0)
     c = lax.broadcasted_iota(jnp.int32, (nz, 2 * nz), 1)
@@ -104,6 +105,9 @@
                   jnp.where((r == cz) & second, -2.0, 0.0)),
     ).astype(jnp.bfloat16)
 
+    def landing(step, side):
+        return halo.at[side, :, rows, :] if step == 0 else arrived.at[step - 1, side]
+
     def halo_copy(step, side):
         if step == 0:
             src = now_hbm.at[:, 0 if side == 0 else width - 1]
@@ -111,7 +115,7 @@
             src = sendbuf.at[step - 1, side]
         return pltpu.make_async_remote_copy(
             src_ref=src,
-            dst_ref=halo.at[step, 1 - side, :, rows, :],
+            dst_ref=landing(step, 1 - side),
             send_sem=hs_sems.at[step, side],
             recv_sem=hr_sems.at[step, 1 - side],
             device_id={"gx": me - 1 if side == 0 else me + 1},
@@ -120,8 +124,8 @@
 
     def halo_arrived(step, side):
         return pltpu.make_async_remote_copy(
-            src_ref=sendbuf.at[0, side],
-            dst_ref=halo.at[step, side, :, rows, :],
+            src_ref=landing(step, side),
+            dst_ref=landing(step, side),
             send_sem=hs_sems.at[step, side],
             recv_sem=hr_sems.at[step, side],
             device_id={"gx": me - 1 if side == 0 else me + 1},
@@ -186,11 +190,13 @@
             @pl.when(has)
             def _(side=side):
                 halo_arrived(step, side).wait_recv()
-        both = [halo[step, side, f, rows, :] for side in range(2) for f in range(2)]
-        outer = jnp.dot(
-            jnp.concatenate(both, axis=0).astype(jnp.bfloat16), zmat[:, nz:],
-            preferred_element_type=F32,
-        )
+        if step == 0:
+            both = halo[:, :, rows, :].reshape(4 * ny, nz).astype(jnp.bfloat16)
+        else:
+            both = arrived[step - 1].reshape(4 * ny, nz)
+        outer = jnp.dot(both, zmat[:, nz:], preferred_element_type=F32)
+        if step > 0:
+            halo[:, :, rows, :] = arrived[step - 1].astype(F32)
         for side in range(2):
             x = 0 if side == 0 else width - 1
             inner = 1 if side == 0 else width - 2
@@ -198,8 +204,8 @@
                 mid, up, dn = [pl.ds(PAD + y + d, EDGE) for d in (0, 1, -1)]
                 cs = [coef[k, x, pl.ds(y, EDGE), :] for k in range(7)]
                 for f in range(2):
-                    a = halo[step, side, f, mid, :]
-                    ya = halo[step, side, f, up, :] - halo[step, side, f, dn, :]
+                    a = halo[side, f, mid, :]
+                    ya = halo[side, f, up, :] - halo[side, f, dn, :]
                     first = (side * 2 + f) * ny + y
                     za = outer[first : first + EDGE]
                     b = now[f, inner, mid, :]
@@ -214,7 +220,7 @@
                     )
                     prv[f, x, mid, :] = acc
                     if step < STEPS - 1:
-                        sendbuf[step, side, f, pl.ds(y, EDGE), :] = acc
+                        sendbuf[step, side, f, pl.ds(y, EDGE), :] = acc.astype(SEND)
         if step < STEPS - 1:
             send_halo(step + 1)
 
@@ -466,8 +472,9 @@
             pltpu.VMEM((nz, 2 * nz), jnp.bfloat16),
             pltpu.VMEM((2, half * ROWS, nz), F32),
             pltpu.VMEM((2, (ny // 2) * half, nz), SEND),
-            pltpu.VMEM((STEPS - 1, 2, 2, ny, nz), F32),
-            pltpu.VMEM((STEPS, 2, 2, ny + 2 * PAD, nz), F32),
+            pltpu.VMEM((STEPS - 1, 2, 2, ny, nz), SEND),
+            pltpu.VMEM((2, 2, ny + 2 * PAD, nz), F32),
+            pltpu.VMEM((STEPS - 1, 2, 2, ny, nz), SEND),
             dma((GROUPS, 5)),
             dma,
             dma,

time: 33.1 us -> 31.1 us (0.940)
  Pallas kernels: 32.9 us -> 30.8 us
    pallas_call x1, Pallas kernels: 26.7 us -> 24.6 us  [local(): pl.pallas_call(functools.partial(wave_kernel, n, jr, cols_per), out_shape...]
where the time goes in v4:
time: 31.1 us; the launch traced here: 30.8 us
  Pallas kernels  30.8 us (99%)
    pallas_call x1, Pallas kernels, local(): pl.pallas_call(functools.partial(wave_kernel, n, jr, cols_per), out_shape...  24.6 us
    pallas_call x1, Pallas kernels, local(): pl.pallas_call(functools.partial(image_kernel, cols_per, jr), grid=(cz //...  6.23 us

profile of v4, /device:TPU:0, one launch (start us, length us, event | category | flops | bytes accessed | tf_op | source)
XLA Modules:
  0.0 30.8 jit_solution(5378381790376378956)
XLA Ops:
  0.0 24.6 %waves.1.cols_ref = bf16[16,2,32,128]{3,2,1,0:T(8,128)(2,1)} custom-call(f32[2,32,64,128]{3,2,1,0:T(8,128)} %now_hbm.1, f32[2,32,64,128]{3,2,1,0:T(8,128)} %prev_hbm.1, bf16[32,64,128]{2,1,0:T(8,128)(2,1)} %eps_hbm.1, bf16[32,64,128]{2,1,0:T(8,128)(2,1)} %tilt_hbm.1, bf16[32,64,128]{2,1,0:T(8,128)(2,1)} %azi_hbm.1, bf16[32,64,128]{2,1,0:T(8,128)(2,1)} %cou_hbm.1), custom_call_target="tpu_custom_call" | custom-call | tf_op jit(solution)/shard_map/waves/pallas_call | solution.py:455
  24.6 6.2 %image.1 = bf16[32,2,128,256]{3,2,1,0:T(8,128)(2,1)} custom-call(s32[32]{0:T(128)} %offsets.1, s32[128]{0:T(128)} %tables_at.1, bf16[16,2,32,128]{3,2,1,0:T(8,128)(2,1)} %waves.1.cols_ref, bf16[4,32,32]{2,1,0:T(8,128)(2,1)} %tab_ref.1), custom_call_target="tpu_custom_call" | custom-call | tf_op jit(solution)/shard_map/image/pallas_call | solution.py:495

commit v5 on v4

--- a/solution.py
+++ b/solution.py
@@ -10,7 +10,7 @@
 LAG_REACH = 16
 PAD = 16
 ROWS = 8
-DEPTH = 32
+DEPTH = 64
 TALL = 16
 EDGE = 32
 GROUPS = 4
@@ -353,7 +353,7 @@
 
 
 def image_kernel(
-    cols_per, jr, offsets, tables_at, cols_ref, tab_ref, out_ref, lines, wide, keep, *prods
+    cols_per, jr, depth, offsets, tables_at, cols_ref, tab_ref, out_ref, lines, wide, keep, *prods
 ):
     n = cols_ref.shape[0]
     half = cols_ref.shape[2] // jr
@@ -387,22 +387,8 @@
     tiles = full // nz
     ta = tables * angles
 
-    sub = lax.broadcasted_iota(jnp.int32, (8, ta), 0)
-    lane_ta = lax.broadcasted_iota(jnp.int32, (angles, 8, ta), 2)
-    row_a = lax.broadcasted_iota(jnp.int32, (angles, 8, ta), 0)
-    weights = []
-    for q in range(DEPTH // 8):
-        row0 = z0 + step * DEPTH + q * 8
-        chosen = jnp.zeros((8, ta), jnp.int32)
-        for c in range(8):
-            chosen = jnp.where(sub == c, tables_at[row0 + c], chosen)
-        wanted = (chosen * angles)[None] + row_a
-        pick = jnp.where(lane_ta == wanted, 1.0, 0.0).reshape(angles * 8, ta)
-        dense = jnp.dot(pick.astype(jnp.bfloat16), wide[...], preferred_element_type=F32)
-        weights.append(dense.astype(jnp.bfloat16) * keep[...])
-
-    lane = lax.broadcasted_iota(jnp.int16, (DEPTH, nz), 1)
-    zero = jnp.zeros((DEPTH, nz), SEND)
+    lane = lax.broadcasted_iota(jnp.int16, (depth, nz), 1)
+    zero = jnp.zeros((depth, nz), SEND)
 
     def moved(parts, d):
         if d == 0:
@@ -418,22 +404,36 @@
             for t in range(tiles)
         ]
 
-    row0 = pl.multiple_of(z0 + step * DEPTH, DEPTH)
+    row0 = pl.multiple_of(z0 + step * depth, depth)
     for j in range(jr):
-        source = [lines[0, j, pl.ds(row0, DEPTH), pl.ds(t * nz, nz)] for t in range(tiles)]
-        receiver = [lines[1, j, pl.ds(row0, DEPTH), pl.ds(t * nz, nz)] for t in range(tiles)]
+        source = [lines[0, j, pl.ds(row0, depth), pl.ds(t * nz, nz)] for t in range(tiles)]
+        receiver = [lines[1, j, pl.ds(row0, depth), pl.ds(t * nz, nz)] for t in range(tiles)]
         for d in range(-LAG_REACH, LAG_REACH):
             left, right = moved(source, d), moved(receiver, -d)
             for t in range(tiles):
                 product = (left[t] * right[t]).astype(F32)
-                for q in range(DEPTH // 8):
-                    prods[j * (DEPTH // 8) + q][d + LAG_REACH, :, pl.ds(t * nz, nz)] = product[8 * q : 8 * q + 8]
+                for q in range(depth // 8):
+                    prods[j * (depth // 8) + q][d + LAG_REACH, :, pl.ds(t * nz, nz)] = product[8 * q : 8 * q + 8]
+
+    sub = lax.broadcasted_iota(jnp.int32, (8, ta), 0)
+    lane_ta = lax.broadcasted_iota(jnp.int32, (angles, 8, ta), 2)
+    row_a = lax.broadcasted_iota(jnp.int32, (angles, 8, ta), 0)
+    weights = []
+    for q in range(depth // 8):
+        row0 = z0 + step * depth + q * 8
+        chosen = jnp.zeros((8, ta), jnp.int32)
+        for c in range(8):
+            chosen = jnp.where(sub == c, tables_at[row0 + c], chosen)
+        wanted = (chosen * angles)[None] + row_a
+        pick = jnp.where(lane_ta == wanted, 1.0, 0.0).reshape(angles * 8, ta)
+        dense = jnp.dot(pick.astype(jnp.bfloat16), wide[...], preferred_element_type=F32)
+        weights.append(dense.astype(jnp.bfloat16) * keep[...])
 
     for j in range(jr):
         results = []
-        for q in range(DEPTH // 8):
+        for q in range(depth // 8):
             lagged = jnp.concatenate(
-                [prods[j * (DEPTH // 8) + q][offsets[h] + LAG_REACH] for h in range(lags)], axis=0
+                [prods[j * (depth // 8) + q][offsets[h] + LAG_REACH] for h in range(lags)], axis=0
             ).astype(jnp.bfloat16)
             total = jnp.dot(weights[q], lagged, preferred_element_type=F32)
             results.append(total.reshape(angles, 8, full))
@@ -492,9 +492,10 @@
     angles, lags = lag_tables.shape[1:]
     tables = lag_tables.shape[0]
     cz = min(cols_per, nz)
+    depth = min(DEPTH, cz)
     image = pl.pallas_call(
-        functools.partial(image_kernel, cols_per, jr),
-        grid=(cz // DEPTH,),
+        functools.partial(image_kernel, cols_per, jr, depth),
+        grid=(cz // depth,),
         out_shape=jax.ShapeDtypeStruct((angles, jr, cz, full), jnp.bfloat16),
         in_specs=[
             pl.BlockSpec(memory_space=pltpu.SMEM),
@@ -502,12 +503,12 @@
             pl.BlockSpec(memory_space=pltpu.VMEM),
             pl.BlockSpec(memory_space=pltpu.VMEM),
         ],
-        out_specs=pl.BlockSpec((angles, jr, DEPTH, full), lambda g: (0, 0, g, 0)),
+        out_specs=pl.BlockSpec((angles, jr, depth, full), lambda g: (0, 0, g, 0)),
         scratch_shapes=[
             pltpu.VMEM((2, jr, nz, full), SEND),
             pltpu.VMEM((tables * angles, lags * 8), jnp.bfloat16),
             pltpu.VMEM((angles * 8, lags * 8), jnp.bfloat16),
-        ] + [pltpu.VMEM((2 * LAG_REACH, 8, full), F32)] * (jr * (DEPTH // 8)),
+        ] + [pltpu.VMEM((2 * LAG_REACH, 8, full), F32)] * (jr * (depth // 8)),
         compiler_params=pltpu.CompilerParams(vmem_limit_bytes=60 << 20),
         name="image",
     )(lag_offsets, table_index, cols, lag_tables)

time: 31.1 us -> 30.7 us (0.987)
  Pallas kernels: 30.8 us -> 30.4 us
    pallas_call x1, Pallas kernels: 6.23 us -> 5.85 us  [local(): pl.pallas_call(functools.partial(image_kernel, cols_per, jr, depth), grid...]
where the time goes in v5:
time: 30.7 us; the launch traced here: 30.4 us
  Pallas kernels  30.4 us (99%)
    pallas_call x1, Pallas kernels, local(): pl.pallas_call(functools.partial(wave_kernel, n, jr, cols_per), out_shape...  24.6 us
    pallas_call x1, Pallas kernels, local(): pl.pallas_call(functools.partial(image_kernel, cols_per, jr, depth), grid...  5.85 us

profile of v5, /device:TPU:0, one launch (start us, length us, event | category | flops | bytes accessed | tf_op | source)
XLA Modules:
  0.0 30.4 jit_solution(16901856709590148240)
XLA Ops:
  0.0 24.6 %waves.1.cols_ref = bf16[16,2,32,128]{3,2,1,0:T(8,128)(2,1)} custom-call(f32[2,32,64,128]{3,2,1,0:T(8,128)} %now_hbm.1, f32[2,32,64,128]{3,2,1,0:T(8,128)} %prev_hbm.1, bf16[32,64,128]{2,1,0:T(8,128)(2,1)} %eps_hbm.1, bf16[32,64,128]{2,1,0:T(8,128)(2,1)} %tilt_hbm.1, bf16[32,64,128]{2,1,0:T(8,128)(2,1)} %azi_hbm.1, bf16[32,64,128]{2,1,0:T(8,128)(2,1)} %cou_hbm.1), custom_call_target="tpu_custom_call" | custom-call | tf_op jit(solution)/shard_map/waves/pallas_call | solution.py:455
  24.6 5.9 %image.1 = bf16[32,2,128,256]{3,2,1,0:T(8,128)(2,1)} custom-call(s32[32]{0:T(128)} %offsets.1, s32[128]{0:T(128)} %tables_at.1, bf16[16,2,32,128]{3,2,1,0:T(8,128)(2,1)} %waves.1.cols_ref, bf16[4,32,32]{2,1,0:T(8,128)(2,1)} %tab_ref.1), custom_call_target="tpu_custom_call" | custom-call | tf_op jit(solution)/shard_map/image/pallas_call | solution.py:496

commit v6 on v5

--- a/solution.py
+++ b/solution.py
@@ -387,6 +387,20 @@
     tiles = full // nz
     ta = tables * angles
 
+    sub = lax.broadcasted_iota(jnp.int32, (8, ta), 0)
+    lane_ta = lax.broadcasted_iota(jnp.int32, (angles, 8, ta), 2)
+    row_a = lax.broadcasted_iota(jnp.int32, (angles, 8, ta), 0)
+    weights = []
+    for q in range(depth // 8):
+        row0 = z0 + step * depth + q * 8
+        chosen = jnp.zeros((8, ta), jnp.int32)
+        for c in range(8):
+            chosen = jnp.where(sub == c, tables_at[row0 + c], chosen)
+        wanted = (chosen * angles)[None] + row_a
+        pick = jnp.where(lane_ta == wanted, 1.0, 0.0).reshape(angles * 8, ta)
+        dense = jnp.dot(pick.astype(jnp.bfloat16), wide[...], preferred_element_type=F32)
+        weights.append(dense.astype(jnp.bfloat16) * keep[...])
+
     lane = lax.broadcasted_iota(jnp.int16, (depth, nz), 1)
     zero = jnp.zeros((depth, nz), SEND)
 
@@ -415,21 +429,6 @@
                 for q in range(depth // 8):
                     prods[j * (depth // 8) + q][d + LAG_REACH, :, pl.ds(t * nz, nz)] = product[8 * q : 8 * q + 8]
 
-    sub = lax.broadcasted_iota(jnp.int32, (8, ta), 0)
-    lane_ta = lax.broadcasted_iota(jnp.int32, (angles, 8, ta), 2)
-    row_a = lax.broadcasted_iota(jnp.int32, (angles, 8, ta), 0)
-    weights = []
-    for q in range(depth // 8):
-        row0 = z0 + step * depth + q * 8
-        chosen = jnp.zeros((8, ta), jnp.int32)
-        for c in range(8):
-            chosen = jnp.where(sub == c, tables_at[row0 + c], chosen)
-        wanted = (chosen * angles)[None] + row_a
-        pick = jnp.where(lane_ta == wanted, 1.0, 0.0).reshape(angles * 8, ta)
-        dense = jnp.dot(pick.astype(jnp.bfloat16), wide[...], preferred_element_type=F32)
-        weights.append(dense.astype(jnp.bfloat16) * keep[...])
-
-    for j in range(jr):
         results = []
         for q in range(depth // 8):
             lagged = jnp.concatenate(

time: 30.7 us -> 30.7 us (level)
  no operation moved by 1% of the time
where the time goes in v6:
time: 30.7 us; the launch traced here: 30.4 us
  Pallas kernels  30.4 us (99%)
    pallas_call x1, Pallas kernels, local(): pl.pallas_call(functools.partial(wave_kernel, n, jr, cols_per), out_shape...  24.6 us
    pallas_call x1, Pallas kernels, local(): pl.pallas_call(functools.partial(image_kernel, cols_per, jr, depth), grid...  5.85 us

profile of v6, /device:TPU:0, one launch (start us, length us, event | category | flops | bytes accessed | tf_op | source)
XLA Modules:
  0.0 30.4 jit_solution(14245768985245541521)
XLA Ops:
  0.0 24.6 %waves.1.cols_ref = bf16[16,2,32,128]{3,2,1,0:T(8,128)(2,1)} custom-call(f32[2,32,64,128]{3,2,1,0:T(8,128)} %now_hbm.1, f32[2,32,64,128]{3,2,1,0:T(8,128)} %prev_hbm.1, bf16[32,64,128]{2,1,0:T(8,128)(2,1)} %eps_hbm.1, bf16[32,64,128]{2,1,0:T(8,128)(2,1)} %tilt_hbm.1, bf16[32,64,128]{2,1,0:T(8,128)(2,1)} %azi_hbm.1, bf16[32,64,128]{2,1,0:T(8,128)(2,1)} %cou_hbm.1), custom_call_target="tpu_custom_call" | custom-call | tf_op jit(solution)/shard_map/waves/pallas_call | solution.py:454
  24.6 5.9 %image.1 = bf16[32,2,128,256]{3,2,1,0:T(8,128)(2,1)} custom-call(s32[32]{0:T(128)} %offsets.1, s32[128]{0:T(128)} %tables_at.1, bf16[16,2,32,128]{3,2,1,0:T(8,128)(2,1)} %waves.1.cols_ref, bf16[4,32,32]{2,1,0:T(8,128)(2,1)} %tab_ref.1), custom_call_target="tpu_custom_call" | custom-call | tf_op jit(solution)/shard_map/image/pallas_call | solution.py:495
